TPU v7x, 512 devices: a whole 4x4x16 slice. The times are simulated.
512 devices in a mesh: rowg: 16 (over y_hi, x, core), colg: 32 (over y_lo, z).
Axes of the slice: x: 4, y: 4 (y_hi: 2, y_lo: 2; y = y_hi * 2 + y_lo), z: 16, core: 2. Of those that a mesh axis runs over, the one named last changes fastest.
Arguments:
- pair_rows: int32 [8192, 32768], P('rowg', 'colg'), may hold values from 0 to 240
- reducers: int32 [2, 1024, 32768], P(None, 'rowg', 'colg'), may hold values from 0 to 240
- pivots: int32 [2, 1024], replicated, may hold values from 0 to 32767, as said below
- counts: int32 [16], replicated, may hold values from 0 to 512, as said below
Outputs:
- reduced: int32 [4096, 32768], P('rowg', 'colg')
Inputs may be any that keep to these rules, and one draw needn't show every extreme that they name: `pivots`: the 2048 pivot columns are all different; column 0 and column 32767 are among them. `counts`: owners 2i and 2i + 1 together hold 512 live rows; some owner has exactly 512 live rows and its partner none; owner 16 - 2 holds more than 256 live rows.
All inputs are finite; a program needn't handle non-finite values.
Results may differ from a plain program's by a relative error of at most 0.000001.
Values may be sent and summed in bfloat16 or wider, within the bound.
No kernel may reach another device: no remote copies, remote signals or barrier semaphores. Data moves between devices by JAX's collectives and lax.ppermute only.
A program may use at most 64 MiB of HBM per device.

v0:
```python
import jax
import jax.numpy as jnp
from jax import lax
from jax.sharding import Mesh, PartitionSpec as P

PANELS = 2
LIVE_DEV = 256
CAP = 96
ROW = ("yh", "x", "core")
COL = ("yl", "z")
modulus = 241.0
half_modulus = 120.0


def centered(values):
    return values - modulus * (values > half_modulus).astype(values.dtype)


def pick_value(table, position):
    marks = lax.iota(jnp.int32, table.shape[0]) == position
    return jnp.sum(jnp.where(marks, table, jnp.zeros_like(table)))


def swap(value, axis):
    return lax.ppermute(value, axis, [(0, 1), (1, 0)])


def take_window(source, start, rows):
    index = start + lax.iota(jnp.int32, rows)
    return jnp.take(source, jnp.clip(index, 0, source.shape[0] - 1), axis=0)


def compact_rows(pair_rows, counts):
    row_index = lax.axis_index(ROW)
    second = lax.axis_index("core")
    first_count = pick_value(counts, row_index - second)
    slots = pair_rows.astype(jnp.float32).astype(jnp.bfloat16)
    keep_start = second * (LIVE_DEV - first_count)
    send_start = jnp.where(second == 0, LIVE_DEV, -first_count)
    kept = take_window(slots, keep_start, LIVE_DEV)
    incoming = swap(take_window(slots, send_start, LIVE_DEV), "core")
    place = lax.iota(jnp.int32, LIVE_DEV)
    mine = jnp.where(second == 0, place < first_count, place >= first_count - LIVE_DEV)
    return jnp.where(mine[:, None], kept, incoming)


def normalize_block(block, own_cols, all_pivots, col_start):
    columns = col_start + lax.iota(jnp.int32, block.shape[1])
    is_pivot = jnp.any(columns[:, None] == all_pivots[None, :], axis=1)
    own_pivot = columns[None, :] == own_cols[:, None]
    entries = centered(block.astype(jnp.float32))
    ones = jnp.ones_like(entries)
    zeros = jnp.zeros_like(entries)
    kept = jnp.where(is_pivot[None, :], jnp.where(own_pivot, ones, zeros), entries)
    return kept.astype(jnp.bfloat16)


def shards(pair_rows, reducers, pivots, counts):
    row_index = lax.axis_index(ROW)
    col_index = lax.axis_index(COL)
    lower = lax.axis_index("yl")
    col_width = pair_rows.shape[1]
    col_start = col_index * col_width
    rows_dev = reducers.shape[1]
    order = pivots.reshape(PANELS, -1, rows_dev).transpose(1, 0, 2).reshape(-1)
    total = order.shape[0]
    own_cols = lax.dynamic_slice_in_dim(order, row_index * PANELS * rows_dev, PANELS * rows_dev)
    normed = normalize_block(
        reducers.reshape(PANELS * rows_dev, col_width), own_cols, order, col_start
    )
    panel = lax.all_gather(normed, ROW, axis=0, tiled=True)
    live = compact_rows(pair_rows, counts)
    owner = order // col_width
    ids = lax.iota(jnp.int32, total)
    same = owner[:, None] == owner[None, :]
    rank = jnp.sum((same & (ids[None, :] < ids[:, None])).astype(jnp.int32), axis=1)
    rounds = jnp.max(rank) // CAP + 1
    z_size = lax.axis_size("z")
    slot = owner % z_size * (2 * CAP) + owner // z_size * CAP

    def fetch(step):
        base = step * CAP
        want = base + lax.iota(jnp.int32, CAP)
        hit = (owner == col_index)[None, :] & (rank[None, :] == want[:, None])
        local = jnp.sum(jnp.where(hit, order[None, :] - col_start + 1, 0), axis=1) - 1
        choose = (local[:, None] == lax.iota(jnp.int32, col_width)[None, :]).astype(jnp.bfloat16)
        mine = lax.dot_general(
            choose, live, (((1,), (1,)), ((), ())), preferred_element_type=jnp.float32
        )
        mine = centered(mine).astype(jnp.bfloat16)
        theirs = swap(mine, "yl")
        both = jnp.where(lower == 0, jnp.stack([mine, theirs]), jnp.stack([theirs, mine]))
        spread = lax.all_gather(both.reshape(2 * CAP, LIVE_DEV), "z", axis=0, tiled=True)
        inside = (rank >= base) & (rank < base + CAP)
        got = jnp.take(spread, jnp.where(inside, slot + rank - base, 0), axis=0)
        return jnp.where(inside[:, None], got, jnp.zeros_like(got))

    half = total // 2

    def reduce_by(result, factors):
        for part in range(2):
            product = lax.dot_general(
                factors[part * half : (part + 1) * half],
                panel[part * half : (part + 1) * half],
                (((0,), (0,)), ((), ())),
                preferred_element_type=jnp.float32,
            )
            result = jnp.mod(result - product, modulus)
        return result

    first = reduce_by(live.astype(jnp.float32), fetch(0)).astype(jnp.int32)
    _, result = lax.while_loop(
        lambda state: state[0] < rounds,
        lambda state: (
            state[0] + 1,
            reduce_by(state[1].astype(jnp.float32), fetch(state[0])).astype(jnp.int32),
        ),
        (jnp.int32(1), first),
    )
    return result


def solution(mesh):
    fine = Mesh(mesh.devices.reshape(2, 4, 2, 2, 16), (*ROW, *COL))
    return jax.shard_map(
        shards,
        mesh=fine,
        in_specs=(P(ROW, COL), P(None, ROW, COL), P(), P()),
        out_specs=P(ROW, COL),
        check_vma=False,
    )
```

profile of v0, /device:TPU:1, one launch (start us, length us, event | category | flops | bytes accessed | tf_op | source)
XLA Modules:
  0.0 193.9 jit_solution(13259388793298008587)
XLA Ops:
  6.5 1.3 fusion.55
  8.5 1.8 convert_convert_fusion
  10.4 1.2 gather_fusion.3
  11.7 8.9 %collective-permute-start.1 = (bf16[256,1024]{1,0:T(8,128)(2,1)S(1)}, bf16[256,1024]{1,0:T(8,128)(2,1)S(1)}, u32[]{:S(2)}, u32[]{:S(2)}) collective-permute-start(bf16[256,1024]{1,0:T(8,128)(2,1)S(1)} %broadcast_select_fusion), channel_id=1, source_target_pairs={{0,32},{32,0},{1,33},{33,1},{2,34},{34,2},{3,35},{35,3},{4,36},{36... | collective-permute-start | bytes 1572872 | tf_op jit(solution)/shard_map/ppermute | solution.py:25
  21.5 4.5 %convert_reduce_fusion = s32[2048]{0:T(1024)S(1)} fusion(s32[2048]{0:T(1024)S(1)} %get-tuple-element.336), kind=kLoop, calls=%fused_computation.34 | loop fusion | flops 20969472 | bytes 16384 | tf_op jit(solution)/shard_map/reduce_sum | solution.py:76
  26.6 1.2 gather_fusion.2
  27.8 0.7 compare_and_fusion.5
  28.4 0.3 select_reduce_fusion.1
  28.7 0.8 copy-done.3
  29.5 1.2 select_select_fusion.2
  30.7 0.3 subtract_convert_fusion.1
  31.0 1.9 collective-permute-start.2
  33.0 3.2 %collective-permute-done.2 = bf16[96,256]{1,0:T(8,128)(2,1)S(1)} collective-permute-done((bf16[96,256]{1,0:T(8,128)(2,1)S(1)}, bf16[96,256]{1,0:T(8,128)(2,1)S(1)}, u32[]{:S(2)}, u32[]{:S(2)}) %collective-permute-start.2) | collective-permute-done | bytes 49184 | tf_op jit(solution)/shard_map/ppermute | solution.py:25
  36.2 0.6 maximum_select_fusion.1
  37.0 1.2 compare_reduce_fusion
  38.2 0.8 fusion.39
  39.1 0.7 reduce_max.9
  41.8 56.7 %all-gather.4.cloned.1.call-done = bf16[3072,256]{1,0:T(8,128)(2,1)} async-done(((bf16[192,256]{1,0:T(8,128)(2,1)}), bf16[3072,256]{1,0:T(8,128)(2,1)}) %all-gather.4.cloned.1.call-update) | async-done | bytes 1572880 | tf_op jit(solution)/shard_map/all_gather | solution.py:93
  98.6 8.2 %gather_fusion.1 = bf16[2048,256]{1,0:T(8,128)(2,1)S(1)} fusion(bf16[3072,256]{1,0:T(8,128)(2,1)} %all-gather.4.cloned.1.call-done, s32[2048]{0:T(1024)S(1)} %broadcast_clamp_fusion.1), kind=kCustom, calls=%fused_computation.3 | custom fusion | bytes 2105344 | tf_op jit(solution)/shard_map/jit(_take)/gather | solution.py:95
  106.8 1.5 select_select_fusion.1
  108.3 72.3 %all-gather.6.cloned.1.call-done = bf16[2048,1024]{1,0:T(8,128)(2,1)} async-done(((bf16[128,1024]{1,0:T(8,128)(2,1)}), bf16[2048,1024]{1,0:T(8,128)(2,1)}) %all-gather.6.cloned.1.call-update) | async-done | bytes 4194320 | tf_op jit(solution)/shard_map/all_gather | solution.py:71
  180.6 2.3 %fusion.26 = f32[256,1024]{1,0:T(8,128)S(1)} fusion(bf16[2048,1024]{1,0:T(8,128)(2,1)} %all-gather.6.cloned.1.call-done, bf16[2048,256]{1,0:T(8,128)(2,1)S(1)} %select_select_fusion.1), kind=kOutput, calls=%fused_computation.40 | convolution fusion | flops 536870912 | bytes 3670016 | tf_op jit(solution)/shard_map/dot_general | solution.py:102
  183.0 3.1 %fusion.30 = s32[256,1024]{1,0:T(8,128)S(1)} fusion(f32[256,1024]{1,0:T(8,128)S(1)} %fusion.26, bf16[256,1024]{1,0:T(8,128)(2,1)S(1)} %select_select_fusion.2, bf16[2048,1024]{1,0:T(8,128)(2,1)} %all-gather.6.cloned.1.call-done, bf16[2048,256]{1,0:T(8,128)(2,1)S(1)} %select_select_fusion.1), kind=kOutput, calls=%fused_computation.47 | convolution fusion | flops 541065216 | bytes 5242880 | tf_op jit(solution)/shard_map/dot_general | solution.py:102
  186.1 1.0 copy-done.1
  (30 shorter events, 0.8 us)
Async XLA Ops:
  6.5 92.0 %all-gather.4.cloned.1.call-start = ((), (), s32[]{:S(2)}) async-start(), calls=%async_computation | async-start | bytes 1671168 | tf_op jit(solution)/shard_map/all_gather | solution.py:93
  8.5 12.7 %copy-start.4 = (s32[2,1024]{1,0:T(2,128)S(1)}, s32[2,1024]{1,0:T(2,128)}, u32[]{:S(2)}) copy-start(s32[2,1024]{1,0:T(2,128)} %param.10) | copy-start | bytes 24580
  11.6 26.6 %copy-start.2 = (s32[2,64,1024]{2,1,0:T(8,128)S(1)}, s32[2,64,1024]{2,1,0:T(8,128)}, u32[]{:S(2)}) copy-start(s32[2,64,1024]{2,1,0:T(8,128)} %param.9) | copy-start | bytes 1572868
  11.7 17.0 %collective-permute-start.1 = (bf16[256,1024]{1,0:T(8,128)(2,1)S(1)}, bf16[256,1024]{1,0:T(8,128)(2,1)S(1)}, u32[]{:S(2)}, u32[]{:S(2)}) collective-permute-start(bf16[256,1024]{1,0:T(8,128)(2,1)S(1)} %broadcast_select_fusion), channel_id=1, source_target_pairs={{0,32},{32,0},{1,33},{33,1},{2,34},{34,2},{3,35},{35,3},{4,36},{36... | collective-permute-start | bytes 1572872 | tf_op jit(solution)/shard_map/ppermute | solution.py:25
  28.7 0.8 copy-start.3
  31.0 5.2 %collective-permute-start.2 = (bf16[96,256]{1,0:T(8,128)(2,1)S(1)}, bf16[96,256]{1,0:T(8,128)(2,1)S(1)}, u32[]{:S(2)}, u32[]{:S(2)}) collective-permute-start(bf16[96,256]{1,0:T(8,128)(2,1)S(1)} %subtract_convert_fusion.1), channel_id=1, source_target_pairs={{0,16},{16,0},{1,17},{17,1},{2,18},{18,2},{3,19},{19,3},{4,20},{20... | collective-permute-start | bytes 147464 | tf_op jit(solution)/shard_map/ppermute | solution.py:25
  36.9 143.8 %all-gather.6.cloned.1.call-start = ((), (), s32[]{:S(2)}) async-start(), calls=%async_computation.1 | async-start | bytes 4456448 | tf_op jit(solution)/shard_map/all_gather | solution.py:71
  186.1 1.0 copy-start.1
Sparse Core Ops, SparseCore 0:
  37.0 61.5 all-gather.3
  101.9 78.7 all-gather.5
where the time goes:
time: 194 us
  waiting for transfers between devices  132 us (68%)
  between operations  17.4 us (9%)
  other arithmetic  14.9 us (8%)
  local copies, waits for them, and re-layouts  12.7 us (7%)
  starting transfers between devices  10.8 us (6%)
  matrix products  5.73 us (3%)
    all_gather x1, waiting for transfers between devices, shards(): panel = lax.all_gather(normed, ROW, axis=0, tiled=True)  72.3 us
    all_gather x1, waiting for transfers between devices, fetch(): lax.all_gather(both.reshape(2 * CAP, LIVE_DEV), 'z', axis=0, tiled=True)  56.7 us
    ppermute x2, starting transfers between devices, swap(): return lax.ppermute(value, axis, [(0, 1), (1, 0)])  10.8 us
    gather x1, local copies, waits for them, and re-layouts, fetch(): got = jnp.take(spread, jnp.where(inside, slot + rank - base, 0), axis=0)  8.24 us
    dot_general x2, matrix products, reduce_by(): lax.dot_general(factors[part * half:(part + 1) * half], panel[part * half...  5.42 us
    reduce_sum x1, other arithmetic, shards(): jnp.sum((same & (ids[None, :] < ids[:, None])).astype(jnp.int32), axis=1)  4.48 us
  transfers between devices with their start and end apart: 4, of which 3 were waited for; matrix products, arithmetic and copies ran while one was open for 10% of the time, Pallas kernels for 0%

commit v1 on v0

--- a/solution.py
+++ b/solution.py
@@ -68,7 +68,9 @@
     normed = normalize_block(
         reducers.reshape(PANELS * rows_dev, col_width), own_cols, order, col_start
     )
-    panel = lax.all_gather(normed, ROW, axis=0, tiled=True)
+    panel = jnp.concatenate(
+        lax.all_to_all(jnp.stack([normed] * lax.axis_size(ROW)), ROW, 0, 0), axis=0
+    )
     live = compact_rows(pair_rows, counts)
     owner = order // col_width
     ids = lax.iota(jnp.int32, total)

time: 194 us -> 174 us (0.90)
  the two profiles are of different devices: /device:TPU:1 before, /device:TPU:8 now
where the time goes in v1:
time: 174 us; the launch traced here: 173 us
  waiting for transfers between devices  108 us (62%)
  between operations  17.5 us (10%)
  local copies, waits for them, and re-layouts  17.1 us (10%)
  starting transfers between devices  14.2 us (8%)
  other arithmetic  13.1 us (8%)
  matrix products  2.75 us (2%)
    all_gather x1, waiting for transfers between devices, fetch(): lax.all_gather(both.reshape(2 * CAP, LIVE_DEV), 'z', axis=0, tiled=True)  76.6 us
    ppermute x2, waiting for transfers between devices, swap(): return lax.ppermute(value, axis, [(0, 1), (1, 0)])  31.9 us
    gather x1, local copies, waits for them, and re-layouts, fetch(): got = jnp.take(spread, jnp.where(inside, slot + rank - base, 0), axis=0)  8.25 us
    ppermute x2, starting transfers between devices, swap(): return lax.ppermute(value, axis, [(0, 1), (1, 0)])  7.87 us
    all_to_all x1, starting transfers between devices, shards(): lax.all_to_all(jnp.stack([normed] * lax.axis_size(ROW)), ROW, 0, 0)  6.29 us
    reduce_sum x1, other arithmetic, shards(): jnp.sum((same & (ids[None, :] < ids[:, None])).astype(jnp.int32), axis=1)  4.48 us
  transfers between devices with their start and end apart: 4, of which 2 were waited for; matrix products, arithmetic and copies ran while one was open for 13% of the time, Pallas kernels for 0%

profile of v1, /device:TPU:8, one launch (start us, length us, event | category | flops | bytes accessed | tf_op | source)
XLA Modules:
  0.0 173.3 jit_solution(5725031537456044209)
XLA Ops:
  6.5 1.3 fusion.51
  8.5 1.8 %convert_convert_fusion = bf16[512,1024]{1,0:T(8,128)(2,1)S(1)} fusion(s32[512,1024]{1,0:T(8,128)} %param.8), kind=kLoop, calls=%fused_computation.38 | loop fusion | flops 1048576 | bytes 3145728 | tf_op jit(solution)/shard_map/convert_element_type | solution.py:37
  10.4 1.2 gather_fusion.3
  11.7 1.9 %collective-permute-start.1 = (bf16[256,1024]{1,0:T(8,128)(2,1)S(1)}, bf16[256,1024]{1,0:T(8,128)(2,1)S(1)}, u32[]{:S(2)}, u32[]{:S(2)}) collective-permute-start(bf16[256,1024]{1,0:T(8,128)(2,1)S(1)} %broadcast_select_fusion), channel_id=1, source_target_pairs={{0,32},{32,0},{1,33},{33,1},{2,34},{34,2},{3,35},{35,3},{4,36},{36... | collective-permute-start | bytes 1572872 | tf_op jit(solution)/shard_map/ppermute | solution.py:25
  13.9 1.2 compare_reduce_fusion
  15.2 2.5 %stack.63 = bf16[16,128,1024]{2,1,0:T(8,128)(2,1)} broadcast(bf16[128,1024]{1,0:T(8,128)(2,1)S(1)} %fusion.35), dimensions={1,2} | broadcast | bytes 4456448 | tf_op jit(solution)/shard_map/stack | solution.py:72
  17.7 6.3 %all-to-all-start = ((bf16[16,128,1024]{2,1,0:T(8,128)(2,1)}), bf16[16,128,1024]{2,1,0:T(8,128)(2,1)}, u32[]{:S(2)}, u32[]{:S(2)}) async-start(bf16[16,128,1024]{2,1,0:T(8,128)(2,1)} %stack.63), calls=%async_computation | async-start | bytes 8388608 | tf_op jit(solution)/shard_map/all_to_all | solution.py:72
  24.8 4.5 %convert_reduce_fusion = s32[2048]{0:T(1024)S(1)} fusion(s32[2048]{0:T(1024)S(1)} %get-tuple-element.338), kind=kLoop, calls=%fused_computation.34 | loop fusion | flops 20969472 | bytes 16384 | tf_op jit(solution)/shard_map/reduce_sum | solution.py:78
  29.9 1.2 gather_fusion.2
  31.1 0.7 compare_and_fusion.5
  31.7 0.3 select_reduce_fusion.1
  32.2 0.3 subtract_convert_fusion.1
  32.5 5.9 %collective-permute-start.2 = (bf16[96,256]{1,0:T(8,128)(2,1)S(1)}, bf16[96,256]{1,0:T(8,128)(2,1)S(1)}, u32[]{:S(2)}, u32[]{:S(2)}) collective-permute-start(bf16[96,256]{1,0:T(8,128)(2,1)S(1)} %subtract_convert_fusion.1), channel_id=1, source_target_pairs={{0,16},{16,0},{1,17},{17,1},{2,18},{18,2},{3,19},{19,3},{4,20},{20... | collective-permute-start | bytes 147464 | tf_op jit(solution)/shard_map/ppermute | solution.py:25
  38.4 31.9 %collective-permute-done.2 = bf16[96,256]{1,0:T(8,128)(2,1)S(1)} collective-permute-done((bf16[96,256]{1,0:T(8,128)(2,1)S(1)}, bf16[96,256]{1,0:T(8,128)(2,1)S(1)}, u32[]{:S(2)}, u32[]{:S(2)}) %collective-permute-start.2) | collective-permute-done | bytes 49184 | tf_op jit(solution)/shard_map/ppermute | solution.py:25
  70.3 0.7 maximum_select_fusion.1
  71.1 0.7 reduce_max.9
  73.8 76.6 %all-gather.3.cloned.1.call-done = bf16[3072,256]{1,0:T(8,128)(2,1)} async-done(((bf16[192,256]{1,0:T(8,128)(2,1)}), bf16[3072,256]{1,0:T(8,128)(2,1)}) %all-gather.3.cloned.1.call-update) | async-done | bytes 1572880 | tf_op jit(solution)/shard_map/all_gather | solution.py:95
  150.4 8.2 %gather_fusion.1 = bf16[2048,256]{1,0:T(8,128)(2,1)S(1)} fusion(bf16[3072,256]{1,0:T(8,128)(2,1)} %all-gather.3.cloned.1.call-done, s32[2048]{0:T(1024)S(1)} %broadcast_clamp_fusion.1), kind=kCustom, calls=%fused_computation.3 | custom fusion | bytes 2105344 | tf_op jit(solution)/shard_map/jit(_take)/gather | solution.py:97
  158.6 1.5 select_select_fusion.1
  160.1 2.7 %fusion.54 = (bf16[8,128,1024]{2,1,0:T(8,128)(2,1)S(1)}, bf16[8,128,1024]{2,1,0:T(8,128)(2,1)S(1)}) fusion(bf16[16,128,1024]{2,1,0:T(8,128)(2,1)} %all-to-all-done), kind=kLoop, calls=%fused_computation.116 | loop fusion | bytes 8388608 | tf_op jit(solution)/shard_map/slice | solution.py:106
  162.8 0.7 fusion.32
  163.6 1.7 fusion.26
  165.3 0.2 while.12
  165.5 1.0 copy-done
  (29 shorter events, 1.0 us)
Async XLA Ops:
  10.4 3.3 %copy-start.2 = (s32[2,1024]{1,0:T(2,128)S(1)}, s32[2,1024]{1,0:T(2,128)}, u32[]{:S(2)}) copy-start(s32[2,1024]{1,0:T(2,128)} %param.10) | copy-start | bytes 24580
  10.4 4.7 %copy-start.1 = (s32[2,64,1024]{2,1,0:T(8,128)S(1)}, s32[2,64,1024]{2,1,0:T(8,128)}, u32[]{:S(2)}) copy-start(s32[2,64,1024]{2,1,0:T(8,128)} %param.9) | copy-start | bytes 1572868
  11.7 20.3 %collective-permute-start.1 = (bf16[256,1024]{1,0:T(8,128)(2,1)S(1)}, bf16[256,1024]{1,0:T(8,128)(2,1)S(1)}, u32[]{:S(2)}, u32[]{:S(2)}) collective-permute-start(bf16[256,1024]{1,0:T(8,128)(2,1)S(1)} %broadcast_select_fusion), channel_id=1, source_target_pairs={{0,32},{32,0},{1,33},{33,1},{2,34},{34,2},{3,35},{35,3},{4,36},{36... | collective-permute-start | bytes 1572872 | tf_op jit(solution)/shard_map/ppermute | solution.py:25
  17.7 142.4 %all-to-all-start = ((bf16[16,128,1024]{2,1,0:T(8,128)(2,1)}), bf16[16,128,1024]{2,1,0:T(8,128)(2,1)}, u32[]{:S(2)}, u32[]{:S(2)}) async-start(bf16[16,128,1024]{2,1,0:T(8,128)(2,1)} %stack.63), calls=%async_computation | async-start | bytes 8388608 | tf_op jit(solution)/shard_map/all_to_all | solution.py:72
  24.0 126.4 %all-gather.3.cloned.1.call-start = ((), (), s32[]{:S(2)}) async-start(), calls=%async_computation.1 | async-start | bytes 1671168 | tf_op jit(solution)/shard_map/all_gather | solution.py:95
  32.5 37.8 %collective-permute-start.2 = (bf16[96,256]{1,0:T(8,128)(2,1)S(1)}, bf16[96,256]{1,0:T(8,128)(2,1)S(1)}, u32[]{:S(2)}, u32[]{:S(2)}) collective-permute-start(bf16[96,256]{1,0:T(8,128)(2,1)S(1)} %subtract_convert_fusion.1), channel_id=1, source_target_pairs={{0,16},{16,0},{1,17},{17,1},{2,18},{18,2},{3,19},{19,3},{4,20},{20... | collective-permute-start | bytes 147464 | tf_op jit(solution)/shard_map/ppermute | solution.py:25
  165.5 1.0 copy-start
Sparse Core Ops, SparseCore 0:
  71.1 79.2 all-gather.2
